TPU v7x, 32 devices: a whole 2x2x4 slice. The times are simulated.
32 devices in a mesh: shot: 16 (over z, y, core), rcv: 2 (over x).
Axes of the slice: x: 2, y: 2, z: 4, core: 2. Of those that a mesh axis runs over, the one named last changes fastest.
Arguments:
- record: bfloat16 [768, 131072], P('rcv', 'shot'), may hold values from -6 to 6
- shot_fire_samples: int32 [512], P('shot'), may hold values from 0 to 131071, as said below
Outputs:
- psf_gram: float32 [2, 4, 768, 768], P(None, None, 'rcv', 'shot')
Inputs may be any that keep to these rules, and one draw needn't show every extreme that they name: `shot_fire_samples`: shot s fires at a sample from s * 256 to s * 256 + 255.
All inputs are finite; a program needn't handle non-finite values.
Results may differ from a plain program's by a relative error of at most 0.0025.
Values may be sent and summed in bfloat16 or wider, within the bound.
A program may use at most 64 MiB of HBM per device.

v0:
```python
import functools
import math

import jax
import jax.numpy as jnp
from jax import lax
from jax.experimental import pallas as pl
from jax.experimental.pallas import tpu as pltpu
from jax.sharding import PartitionSpec as P

WIN = 2048
SPACING = 256


freq_bins = (24, 40, 56, 80)


def shifted(block, axis, distance):
    devices = range(lax.axis_size(axis))
    route = [(i - distance, i) for i in devices if i - distance in devices]
    return lax.ppermute(block, axis, route)


def dft_table(window_len):
    lag_index = jnp.arange(window_len, dtype=jnp.int32)
    bin_list = jnp.array(freq_bins, dtype=jnp.int32)
    turn_count = lag_index[:, None] * bin_list[None, :] % window_len
    phase_angle = 2.0 * math.pi / window_len * turn_count.astype(jnp.float32)
    dft_rows = jnp.concatenate([jnp.cos(phase_angle), -jnp.sin(phase_angle)], axis=1) / math.sqrt(
        window_len
    )
    return dft_rows.astype(jnp.bfloat16)


def shifted_tables(jitter, span):
    lag_index = jnp.arange(span, dtype=jnp.int32)[None, :] - jitter[:, None]
    inside = (lag_index >= 0) & (lag_index < WIN)
    clipped = jnp.clip(lag_index, 0, WIN - 1)
    bin_list = jnp.array(freq_bins, dtype=jnp.int32)
    turn_count = clipped[:, None, :] * bin_list[None, :, None] % WIN
    phase_angle = 2.0 * math.pi / WIN * turn_count.astype(jnp.float32)
    table = jnp.concatenate([jnp.cos(phase_angle), -jnp.sin(phase_angle)], axis=1) / math.sqrt(WIN)
    table = jnp.where(inside[:, None, :], table, 0.0)
    return table.astype(jnp.bfloat16)


def local_spectra(extended, sample_offsets, dft_rows):
    count_of_shots = sample_offsets.shape[0]
    reach_blocks = WIN // SPACING + 1
    jitter = sample_offsets - jnp.arange(count_of_shots, dtype=jnp.int32) * SPACING
    tables = shifted_tables(jitter, reach_blocks * SPACING)
    tables = tables.reshape(count_of_shots, dft_rows.shape[1], reach_blocks, SPACING)
    blocks = extended.reshape(extended.shape[0], extended.shape[1] // SPACING, SPACING)
    total = jnp.zeros((count_of_shots, dft_rows.shape[1], extended.shape[0]), jnp.float32)
    for offset in range(reach_blocks):
        record_part = blocks[:, offset : offset + count_of_shots, :]
        total = total + jnp.einsum(
            "rsu,scu->scr", record_part, tables[:, :, offset, :], preferred_element_type=jnp.float32
        )
    return total


def gram_terms(left, right):
    nfreq = len(freq_bins)
    left_re = left[:, :nfreq, :]
    left_im = left[:, nfreq:, :]
    right_re = right[:, :nfreq, :]
    right_im = right[:, nfreq:, :]
    gram_real = jnp.einsum("sfr,sfq->frq", left_re, right_re, preferred_element_type=jnp.float32)
    gram_real = gram_real + jnp.einsum(
        "sfr,sfq->frq", left_im, right_im, preferred_element_type=jnp.float32
    )
    gram_imag = jnp.einsum("sfr,sfq->frq", left_re, right_im, preferred_element_type=jnp.float32)
    gram_imag = gram_imag - jnp.einsum(
        "sfr,sfq->frq", left_im, right_re, preferred_element_type=jnp.float32
    )
    return jnp.stack([gram_real, gram_imag], axis=0)


def per_device(record, shot_fire_samples):
    trace_segment_length = record.shape[1]
    count_of_shots = shot_fire_samples.shape[0]
    dft_rows = dft_table(WIN)
    sample_offsets = shot_fire_samples - lax.axis_index("shot") * trace_segment_length
    head_rows = record[:, :WIN]
    rim_rows = shifted(head_rows, "shot", -1)
    extended = jnp.concatenate([record, rim_rows], axis=1)
    trace_spectra = local_spectra(extended, sample_offsets, dft_rows)
    trace_spectra = trace_spectra.astype(jnp.bfloat16)
    all_receivers = lax.all_gather(trace_spectra, "rcv", axis=2, tiled=True)
    total_shots = count_of_shots * lax.axis_size("shot")
    row_side = lax.all_gather(trace_spectra, "shot", axis=0, tiled=True)
    column_side = lax.all_to_all(all_receivers, "shot", split_axis=2, concat_axis=0, tiled=True)
    result = gram_terms(row_side, column_side)
    return result / total_shots


LANES = 128
HALF = 16
GROUP = 8
MESH = pl.DeviceIdType.MESH


def lane_fields(shape):
    lane = lax.broadcasted_iota(jnp.int32, shape, len(shape) - 1)
    return lane // 32 % 4, lane // 16 % 2, lane % 16


def rotated(lag):
    freq, part, _ = lane_fields((1, LANES))
    bins = jnp.full((1, LANES), freq_bins[0], jnp.int32)
    for f in range(1, len(freq_bins)):
        bins = jnp.where(freq == f, freq_bins[f], bins)
    turn = (lag & (SPACING - 1)) * bins + part * (WIN // 4)
    turn = ((turn + WIN // 2) & (WIN - 1)) - WIN // 2
    x = (math.pi / WIN) * turn.astype(jnp.float32)
    y = x * x
    series = 1.0 / math.factorial(13)
    for k in (11, 9, 7, 5, 3, 1):
        series = series * y + (-1.0) ** (k // 2) / math.factorial(k)
    half_sine = x * series
    return (1.0 - 2.0 * half_sine * half_sine) / math.sqrt(WIN)


def kernel(
    n, fire_hbm, rec_ref, out_ref,
    fire_ref, fire_sem, rec, joff, poff, table, tmask, rim_out, rim_in, gat, col, rmat, acc,
    rec_sem, jit_sem, rim_sem, ring_send, pair_send, chunk_recv, col_send, col_recv,
):
    me = lax.axis_index("shot")
    mj = lax.axis_index("rcv")
    rows = rec.shape[0]
    span = GROUP * SPACING
    chips = n // 2
    nz = chips // 2
    ncol = col.shape[2]
    shift, reach = SPACING.bit_length() - 1, WIN // SPACING
    core = me % 2
    chip = me // 2
    z, y = chip // 2, chip % 2
    pos = jnp.where(y == 0, z, chips - 1 - z)

    def device_at(position, which):
        q = (position + 2 * chips) % chips
        second = q >= nz
        zz = jnp.where(second, chips - 1 - q, q)
        yy = jnp.where(second, 1, 0)
        return (zz * 2 + yy) * 2 + which

    cw, ccw = device_at(pos + 1, core), device_at(pos - 1, core)
    pair = chip * 2 + (1 - core)
    prev, nxt = (me + n - 1) % n, (me + 1) % n

    def load(g):
        part = pl.ds(g * span, span)
        return pltpu.make_async_copy(rec_ref.at[:, part], rec.at[:, part], rec_sem.at[g])

    fires = pltpu.make_async_copy(fire_hbm, fire_ref, fire_sem)
    fires.start()
    for g in (1, 2, 0, 3):
        load(g).start()

    barrier = pltpu.get_barrier_semaphore()
    for other in (cw, ccw, pair, prev, nxt):
        pl.semaphore_signal(barrier, inc=1, device_id=(other, mj), device_id_type=MESH)
    pl.semaphore_signal(barrier, inc=1, device_id=(me, 1 - mj), device_id_type=MESH)
    fires.wait()
    _, _, shot_lane = lane_fields((1, LANES))
    offs = []
    for h in range(2):
        row = jnp.zeros((1, LANES), jnp.int32)
        for s in range(HALF):
            row = jnp.where(shot_lane == s, fire_ref[h * HALF + s], row)
        offs.append(row - me * rec.shape[1])
    joff[...] = jnp.broadcast_to(offs[1], joff.shape)

    jitter = pltpu.make_async_remote_copy(
        joff, poff, jit_sem.at[0], jit_sem.at[1], device_id=(nxt, mj), device_id_type=MESH
    )

    def fill_tables(kind, off_row):
        u = lax.broadcasted_iota(jnp.int32, (SPACING, LANES), 0)
        start = off_row & (SPACING - 1)
        value = rotated(u - start)
        table[kind, 0] = jnp.where(u >= start, value, 0.0).astype(jnp.bfloat16)
        table[kind, 1] = jnp.where(u < start, value, 0.0).astype(jnp.bfloat16)

    def group_dot(g, kinds):
        for slot, (kind, off_row) in enumerate(kinds):
            block_of = jnp.broadcast_to(off_row >> shift, (16, LANES))
            lanes = slice(slot * LANES, (slot + 1) * LANES)
            for b in range(GROUP):
                order = g * GROUP + b - block_of
                early = ((order >= 0) & (order < reach)).astype(jnp.float32).astype(jnp.bfloat16)
                late = ((order >= 1) & (order <= reach)).astype(jnp.float32).astype(jnp.bfloat16)
                block = (SPACING // 16, 16, LANES)
                mixed = table[kind, 0].reshape(block) * early + table[kind, 1].reshape(block) * late
                tmask[b * SPACING : (b + 1) * SPACING, lanes] = mixed.reshape(SPACING, LANES)
        return jnp.dot(
            rec[:, g * span : (g + 1) * span], tmask[:, : len(kinds) * LANES],
            preferred_element_type=jnp.float32,
        )

    def ring(src, h, d):
        return pltpu.make_async_remote_copy(
            gat.at[src, h], gat.at[src, h], ring_send.at[d, src, h], chunk_recv.at[src, h],
            device_id=(cw if d == 0 else ccw, mj), device_id_type=MESH,
        )

    def share(src, h):
        return pltpu.make_async_remote_copy(
            gat.at[src, h], gat.at[src, h], pair_send.at[src, h], chunk_recv.at[src, h],
            device_id=(pair, mj), device_id_type=MESH,
        )

    home = me * ncol // rows
    provider = home == mj
    first = pl.multiple_of(jnp.where(provider, me * ncol - home * rows, 0), 16)

    def col_far(src, h):
        return pltpu.make_async_remote_copy(
            gat.at[src, h, pl.ds(first, ncol), :], col.at[src, h], col_send.at[src, h],
            col_recv.at[src, h], device_id=(me, 1 - mj), device_id_type=MESH,
        )

    def col_near(src, h):
        return pltpu.make_async_copy(
            gat.at[src, h, pl.ds(first, ncol), :], col.at[src, h], col_recv.at[src, h]
        )

    def send_col(src, h):
        @pl.when(provider)
        def _():
            col_far(src, h).start()
            col_near(src, h).start()

    def send_own(h):
        ring(me, h, h).start()
        ring(me, h, 1 - h).start()
        share(me, h).start()
        send_col(me, h)

    def gram(src):
        for h in range(2):
            x = col[src, h].astype(jnp.float32)
            freq, part, _ = lane_fields(x.shape)
            swapped = jnp.where(part == 0, pltpu.roll(x, LANES - 16, 1), -pltpu.roll(x, 16, 1))
            for ri, value in enumerate((x, swapped)):
                for f in range(4):
                    rmat[pl.ds((ri * 4 + f) * ncol, ncol), h * LANES : (h + 1) * LANES] = jnp.where(
                        freq == f, value, 0.0
                    ).astype(jnp.bfloat16)
        left = jnp.concatenate([gat[src, 0], gat[src, 1]], axis=1)
        acc[...] += lax.dot_general(
            rmat[...], left, (((1,), (1,)), ((), ())), preferred_element_type=jnp.float32
        )

    fill_tables(0, offs[0])
    fill_tables(1, offs[1])
    acc[...] = jnp.zeros_like(acc)
    kinds = ((0, offs[0]), (1, offs[1]))
    load(1).wait()
    own = group_dot(1, kinds[:1])
    pl.semaphore_wait(barrier, 6)
    jitter.start()
    load(2).wait()
    both = group_dot(2, kinds)
    load(0).wait()
    own = own + both[:, :LANES] + group_dot(0, kinds[:1])
    gat[me, 0] = own.astype(jnp.bfloat16)
    send_own(0)
    jitter.wait()
    offp = poff[0:1, :] - rec.shape[1]
    fill_tables(2, offp)
    foreign = group_dot(0, ((2, offp),))
    cut = rows // 2
    rim_out[...] = foreign[:cut] + pltpu.roll(foreign[cut:], LANES - 8, 1)
    rim = pltpu.make_async_remote_copy(
        rim_out, rim_in, rim_sem.at[0], rim_sem.at[1], device_id=(prev, mj), device_id_type=MESH
    )
    rim.start()
    load(3).wait()
    second = both[:, LANES:] + group_dot(3, kinds[1:])
    rim.wait()
    _, _, shot = lane_fields((cut, LANES))
    wanted = (shot >= 8) & (me < n - 1)
    upper = jnp.where(wanted, rim_in[...], 0.0)
    lower = jnp.where(wanted, pltpu.roll(rim_in[...], 8, 1), 0.0)
    gat[me, 1, :cut] = (second[:cut] + upper).astype(jnp.bfloat16)
    gat[me, 1, cut:] = (second[cut:] + lower).astype(jnp.bfloat16)
    send_own(1)

    half = chips // 2

    def hops(h, d):
        return half if h == d else half - 1

    def arrivals(t):
        found = []
        for h in range(2):
            for d in range(2):
                if 1 <= t <= hops(h, d):
                    found.append((h, d))
        return found

    def source(t, d, which):
        return device_at(pos - t if d == 0 else pos + t, which)

    def step_sources(t):
        if t == 0:
            return [0]
        return [0, 1] if t < half else [0]

    def gram_step(t):
        for which in (core, 1 - core):
            for d in step_sources(t):
                src = source(t, d, which)
                for h in range(2):
                    col_near(src, h).wait()
                gram(src)

    for t in range(half + 1):
        for h, d in arrivals(t):
            src = source(t, d, core)
            ring(src, h, d).wait_recv()
            if t < hops(h, d):
                ring(src, h, d).start()
            share(src, h).start()
            send_col(src, h)
        if t > 0:
            gram_step(t - 1)
        for d in step_sources(t):
            for h in range(2):
                src = source(t, d, 1 - core)
                share(src, h).wait_recv()
                send_col(src, h)
    gram_step(half)

    scale = 1.0 / (n * 2 * HALF)
    for g in range(8):
        out_ref[g // 4, g % 4] = acc[g * ncol : (g + 1) * ncol, :] * scale

    for h in range(2):
        ring(me, h, 0).wait_send()
        ring(me, h, 1).wait_send()
    for t in range(1, half + 1):
        for h, d in arrivals(t):
            src = source(t, d, core)
            if t < hops(h, d):
                ring(src, h, d).wait_send()
            share(src, h).wait_send()
    for h in range(2):
        share(me, h).wait_send()

    @pl.when(provider)
    def _():
        for src in range(n):
            for h in range(2):
                col_far(src, h).wait_send()


def fused_device(n, ncol, record, shot_fire_samples):
    rows, length = record.shape
    gram = pl.pallas_call(
        functools.partial(kernel, n),
        out_shape=jax.ShapeDtypeStruct((2, 4, ncol, rows), jnp.float32),
        in_specs=[
            pl.BlockSpec(memory_space=pltpu.HBM),
            pl.BlockSpec(memory_space=pltpu.HBM),
        ],
        out_specs=pl.BlockSpec(memory_space=pltpu.VMEM),
        scratch_shapes=[
            pltpu.SMEM(shot_fire_samples.shape, jnp.int32),
            pltpu.SemaphoreType.DMA,
            pltpu.VMEM((rows, length), jnp.bfloat16),
            pltpu.VMEM((8, LANES), jnp.int32),
            pltpu.VMEM((8, LANES), jnp.int32),
            pltpu.VMEM((3, 2, SPACING, LANES), jnp.bfloat16),
            pltpu.VMEM((GROUP * SPACING, 2 * LANES), jnp.bfloat16),
            pltpu.VMEM((rows // 2, LANES), jnp.float32),
            pltpu.VMEM((rows // 2, LANES), jnp.float32),
            pltpu.VMEM((n, 2, rows, LANES), jnp.bfloat16),
            pltpu.VMEM((n, 2, ncol, LANES), jnp.bfloat16),
            pltpu.VMEM((8 * ncol, 2 * LANES), jnp.bfloat16),
            pltpu.VMEM((8 * ncol, rows), jnp.float32),
            pltpu.SemaphoreType.DMA((length // (GROUP * SPACING),)),
            pltpu.SemaphoreType.DMA((2,)),
            pltpu.SemaphoreType.DMA((2,)),
            pltpu.SemaphoreType.DMA((2, n, 2)),
            pltpu.SemaphoreType.DMA((n, 2)),
            pltpu.SemaphoreType.DMA((n, 2)),
            pltpu.SemaphoreType.DMA((n, 2)),
            pltpu.SemaphoreType.DMA((n, 2)),
        ],
        compiler_params=pltpu.CompilerParams(
            collective_id=0, has_side_effects=True, vmem_limit_bytes=50 * 1024 * 1024
        ),
    )(shot_fire_samples, record)
    return gram.transpose(0, 1, 3, 2)


def whole_step(n, receivers, record, shot_fire_samples):
    rows, length = record.shape
    shots = shot_fire_samples.shape[0]
    ncol = receivers // n
    fits = (
        receivers == 2 * rows and ncol % 16 == 0 and rows % (2 * ncol) == 0
        and shots == 2 * HALF and length == shots * SPACING and n % 8 == 0
    )
    if fits:
        return fused_device(n, ncol, record, shot_fire_samples)
    return per_device(record, shot_fire_samples)


def solution(mesh):
    def step(record, shot_fire_samples):
        body = functools.partial(whole_step, mesh.shape["shot"], record.shape[0])
        return jax.shard_map(
            body,
            mesh=mesh,
            in_specs=(P("rcv", "shot"), P("shot")),
            out_specs=P(None, None, "rcv", "shot"),
            check_vma=False,
        )(record, shot_fire_samples)

    return step
```

profile of v0, /device:TPU:0, one launch (start us, length us, event | category | flops | bytes accessed | tf_op | source)
XLA Modules:
  0.0 34.4 jit_solution(11351892366168523700)
XLA Ops:
  0.0 0.0 copy-start
  0.0 0.7 %copy-done = s32[32]{0:T(128)S(1)} copy-done((s32[32]{0:T(128)S(1)}, s32[32]{0:T(128)}, u32[]{:S(2)}) %copy-start) | copy-done | bytes 152
  0.7 32.9 %shard_map.28 = f32[2,4,48,384]{3,2,1,0:T(8,128)S(1)} custom-call(s32[32]{0:T(128)S(1)} %copy-done, bf16[384,8192]{1,0:T(8,128)(2,1)} %rec_ref.1), custom_call_target="tpu_custom_call" | custom-call | tf_op jit(solution)/shard_map/pallas_call | solution.py:364
  33.6 0.8 %copy.4 = f32[2,4,384,48]{2,3,1,0:T(8,128)} copy(f32[2,4,384,48]{2,3,1,0:T(8,128)S(1)} %bitcast.1) | data formatting | bytes 1179648
Async XLA Ops:
  0.0 0.7 %copy-start = (s32[32]{0:T(128)S(1)}, s32[32]{0:T(128)}, u32[]{:S(2)}) copy-start(s32[32]{0:T(128)} %fire_hbm.1) | copy-start | bytes 388
where the time goes:
time: 35.1 us; the launch traced here: 34.4 us
  Pallas kernels  32.9 us (94%)
  local copies, waits for them, and re-layouts  1.47 us (4%)
    pallas_call x1, Pallas kernels, fused_device(): pl.pallas_call(functools.partial(kernel, n), out_shape=jax.ShapeDtypeStru...  32.9 us
    unnamed x3, local copies, waits for them, and re-layouts  1.47 us

commit v1 on v0

--- a/solution.py
+++ b/solution.py
@@ -149,7 +149,7 @@
 
     cw, ccw = device_at(pos + 1, core), device_at(pos - 1, core)
     pair = chip * 2 + (1 - core)
-    prev, nxt = (me + n - 1) % n, (me + 1) % n
+    prev, nxt = jnp.maximum(me - 1, 0), jnp.minimum(me + 1, n - 1)
 
     def load(g):
         part = pl.ds(g * span, span)
@@ -161,9 +161,16 @@
         load(g).start()
 
     barrier = pltpu.get_barrier_semaphore()
-    for other in (cw, ccw, pair, prev, nxt):
-        pl.semaphore_signal(barrier, inc=1, device_id=(other, mj), device_id_type=MESH)
-    pl.semaphore_signal(barrier, inc=1, device_id=(me, 1 - mj), device_id_type=MESH)
+    has_prev, has_next = me > 0, me < n - 1
+
+    def greet(other, column):
+        pl.semaphore_signal(barrier, inc=1, device_id=(other, column), device_id_type=MESH)
+
+    for other in (cw, ccw, pair):
+        greet(other, mj)
+    greet(me, 1 - mj)
+    pl.when(has_prev)(lambda: greet(prev, mj))
+    pl.when(has_next)(lambda: greet(nxt, mj))
     fires.wait()
     _, _, shot_lane = lane_fields((1, LANES))
     offs = []
@@ -173,6 +180,10 @@
             row = jnp.where(shot_lane == s, fire_ref[h * HALF + s], row)
         offs.append(row - me * rec.shape[1])
     joff[...] = jnp.broadcast_to(offs[1], joff.shape)
+
+    @pl.when(me == 0)
+    def _():
+        poff[...] = jnp.zeros_like(poff)
 
     jitter = pltpu.make_async_remote_copy(
         joff, poff, jit_sem.at[0], jit_sem.at[1], device_id=(nxt, mj), device_id_type=MESH
@@ -203,13 +214,13 @@
 
     def ring(src, h, d):
         return pltpu.make_async_remote_copy(
-            gat.at[src, h], gat.at[src, h], ring_send.at[d, src, h], chunk_recv.at[src, h],
+            gat.at[src, h], gat.at[src, h], ring_send, chunk_recv.at[src, h],
             device_id=(cw if d == 0 else ccw, mj), device_id_type=MESH,
         )
 
     def share(src, h):
         return pltpu.make_async_remote_copy(
-            gat.at[src, h], gat.at[src, h], pair_send.at[src, h], chunk_recv.at[src, h],
+            gat.at[src, h], gat.at[src, h], pair_send, chunk_recv.at[src, h],
             device_id=(pair, mj), device_id_type=MESH,
         )
 
@@ -219,7 +230,7 @@
 
     def col_far(src, h):
         return pltpu.make_async_remote_copy(
-            gat.at[src, h, pl.ds(first, ncol), :], col.at[src, h], col_send.at[src, h],
+            gat.at[src, h, pl.ds(first, ncol), :], col.at[src, h], col_send,
             col_recv.at[src, h], device_id=(me, 1 - mj), device_id_type=MESH,
         )
 
@@ -261,15 +272,15 @@
     kinds = ((0, offs[0]), (1, offs[1]))
     load(1).wait()
     own = group_dot(1, kinds[:1])
-    pl.semaphore_wait(barrier, 6)
-    jitter.start()
+    pl.semaphore_wait(barrier, 4 + has_prev.astype(jnp.int32) + has_next.astype(jnp.int32))
+    pl.when(has_next)(jitter.start)
     load(2).wait()
     both = group_dot(2, kinds)
     load(0).wait()
     own = own + both[:, :LANES] + group_dot(0, kinds[:1])
     gat[me, 0] = own.astype(jnp.bfloat16)
     send_own(0)
-    jitter.wait()
+    pl.when(has_prev)(jitter.wait_recv)
     offp = poff[0:1, :] - rec.shape[1]
     fill_tables(2, offp)
     foreign = group_dot(0, ((2, offp),))
@@ -278,10 +289,10 @@
     rim = pltpu.make_async_remote_copy(
         rim_out, rim_in, rim_sem.at[0], rim_sem.at[1], device_id=(prev, mj), device_id_type=MESH
     )
-    rim.start()
+    pl.when(has_prev)(rim.start)
     load(3).wait()
     second = both[:, LANES:] + group_dot(3, kinds[1:])
-    rim.wait()
+    pl.when(has_next)(rim.wait_recv)
     _, _, shot = lane_fields((cut, LANES))
     wanted = (shot >= 8) & (me < n - 1)
     upper = jnp.where(wanted, rim_in[...], 0.0)
@@ -340,27 +351,19 @@
     for g in range(8):
         out_ref[g // 4, g % 4] = acc[g * ncol : (g + 1) * ncol, :] * scale
 
-    for h in range(2):
-        ring(me, h, 0).wait_send()
-        ring(me, h, 1).wait_send()
-    for t in range(1, half + 1):
-        for h, d in arrivals(t):
-            src = source(t, d, core)
-            if t < hops(h, d):
-                ring(src, h, d).wait_send()
-            share(src, h).wait_send()
-    for h in range(2):
-        share(me, h).wait_send()
-
-    @pl.when(provider)
-    def _():
-        for src in range(n):
-            for h in range(2):
-                col_far(src, h).wait_send()
+    def drain(buffer, sem):
+        pltpu.make_async_copy(buffer, buffer, sem).wait()
+
+    pl.when(has_next)(jitter.wait_send)
+    pl.when(has_prev)(rim.wait_send)
+    drain(gat.at[pl.ds(0, chips - 1)], ring_send)
+    drain(gat.at[pl.ds(0, chips)], pair_send)
+    pl.when(provider)(lambda: drain(col, col_send))
 
 
 def fused_device(n, ncol, record, shot_fire_samples):
     rows, length = record.shape
+    shot_fire_samples = pltpu.with_memory_space_constraint(shot_fire_samples, pltpu.HBM)
     gram = pl.pallas_call(
         functools.partial(kernel, n),
         out_shape=jax.ShapeDtypeStruct((2, 4, ncol, rows), jnp.float32),
@@ -386,10 +389,10 @@
             pltpu.SemaphoreType.DMA((length // (GROUP * SPACING),)),
             pltpu.SemaphoreType.DMA((2,)),
             pltpu.SemaphoreType.DMA((2,)),
-            pltpu.SemaphoreType.DMA((2, n, 2)),
+            pltpu.SemaphoreType.DMA,
+            pltpu.SemaphoreType.DMA,
             pltpu.SemaphoreType.DMA((n, 2)),
-            pltpu.SemaphoreType.DMA((n, 2)),
-            pltpu.SemaphoreType.DMA((n, 2)),
+            pltpu.SemaphoreType.DMA,
             pltpu.SemaphoreType.DMA((n, 2)),
         ],
         compiler_params=pltpu.CompilerParams(

time: 35.1 us -> 33.4 us (0.952); the launches traced: 34.4 us -> 33.3 us
  local copies, waits for them, and re-layouts: 1.47 us -> 0.82 us
  Pallas kernels: 32.9 us -> 32.4 us
    unnamed x3 -> x1, local copies, waits for them, and re-layouts: 1.47 us -> 0.82 us
    pallas_call x1, Pallas kernels: 32.9 us -> 32.4 us  [fused_device(): pl.pallas_call(functools.partial(kernel, n), out_shape=jax.ShapeDtypeStru...]
where the time goes in v1:
time: 33.4 us; the launch traced here: 33.3 us
  Pallas kernels  32.4 us (97%)
  local copies, waits for them, and re-layouts  0.82 us (2%)
    pallas_call x1, Pallas kernels, fused_device(): pl.pallas_call(functools.partial(kernel, n), out_shape=jax.ShapeDtypeStru...  32.4 us
    unnamed x1, local copies, waits for them, and re-layouts  0.82 us

profile of v1, /device:TPU:0, one launch (start us, length us, event | category | flops | bytes accessed | tf_op | source)
XLA Modules:
  0.0 33.3 jit_solution(7536309626127300015)
XLA Ops:
  0.0 32.4 %shard_map.28 = f32[2,4,48,384]{3,2,1,0:T(8,128)S(1)} custom-call(s32[32]{0:T(128)} %fire_hbm.1, bf16[384,8192]{1,0:T(8,128)(2,1)} %rec_ref.1), custom_call_target="tpu_custom_call" | custom-call | tf_op jit(solution)/shard_map/pallas_call | solution.py:367
  32.5 0.8 %copy.4 = f32[2,4,384,48]{2,3,1,0:T(8,128)} copy(f32[2,4,384,48]{2,3,1,0:T(8,128)S(1)} %bitcast.1) | data formatting | bytes 1179648

commit v2 on v1

v2 whole, which is shorter than its diff:
```python
import functools
import math

import jax
import jax.numpy as jnp
from jax import lax
from jax.experimental import pallas as pl
from jax.experimental.pallas import tpu as pltpu
from jax.sharding import PartitionSpec as P

WIN = 2048
SPACING = 256


freq_bins = (24, 40, 56, 80)


def shifted(block, axis, distance):
    devices = range(lax.axis_size(axis))
    route = [(i - distance, i) for i in devices if i - distance in devices]
    return lax.ppermute(block, axis, route)


def dft_table(window_len):
    lag_index = jnp.arange(window_len, dtype=jnp.int32)
    bin_list = jnp.array(freq_bins, dtype=jnp.int32)
    turn_count = lag_index[:, None] * bin_list[None, :] % window_len
    phase_angle = 2.0 * math.pi / window_len * turn_count.astype(jnp.float32)
    dft_rows = jnp.concatenate([jnp.cos(phase_angle), -jnp.sin(phase_angle)], axis=1) / math.sqrt(
        window_len
    )
    return dft_rows.astype(jnp.bfloat16)


def shifted_tables(jitter, span):
    lag_index = jnp.arange(span, dtype=jnp.int32)[None, :] - jitter[:, None]
    inside = (lag_index >= 0) & (lag_index < WIN)
    clipped = jnp.clip(lag_index, 0, WIN - 1)
    bin_list = jnp.array(freq_bins, dtype=jnp.int32)
    turn_count = clipped[:, None, :] * bin_list[None, :, None] % WIN
    phase_angle = 2.0 * math.pi / WIN * turn_count.astype(jnp.float32)
    table = jnp.concatenate([jnp.cos(phase_angle), -jnp.sin(phase_angle)], axis=1) / math.sqrt(WIN)
    table = jnp.where(inside[:, None, :], table, 0.0)
    return table.astype(jnp.bfloat16)


def local_spectra(extended, sample_offsets, dft_rows):
    count_of_shots = sample_offsets.shape[0]
    reach_blocks = WIN // SPACING + 1
    jitter = sample_offsets - jnp.arange(count_of_shots, dtype=jnp.int32) * SPACING
    tables = shifted_tables(jitter, reach_blocks * SPACING)
    tables = tables.reshape(count_of_shots, dft_rows.shape[1], reach_blocks, SPACING)
    blocks = extended.reshape(extended.shape[0], extended.shape[1] // SPACING, SPACING)
    total = jnp.zeros((count_of_shots, dft_rows.shape[1], extended.shape[0]), jnp.float32)
    for offset in range(reach_blocks):
        record_part = blocks[:, offset : offset + count_of_shots, :]
        total = total + jnp.einsum(
            "rsu,scu->scr", record_part, tables[:, :, offset, :], preferred_element_type=jnp.float32
        )
    return total


def gram_terms(left, right):
    nfreq = len(freq_bins)
    left_re = left[:, :nfreq, :]
    left_im = left[:, nfreq:, :]
    right_re = right[:, :nfreq, :]
    right_im = right[:, nfreq:, :]
    gram_real = jnp.einsum("sfr,sfq->frq", left_re, right_re, preferred_element_type=jnp.float32)
    gram_real = gram_real + jnp.einsum(
        "sfr,sfq->frq", left_im, right_im, preferred_element_type=jnp.float32
    )
    gram_imag = jnp.einsum("sfr,sfq->frq", left_re, right_im, preferred_element_type=jnp.float32)
    gram_imag = gram_imag - jnp.einsum(
        "sfr,sfq->frq", left_im, right_re, preferred_element_type=jnp.float32
    )
    return jnp.stack([gram_real, gram_imag], axis=0)


def per_device(record, shot_fire_samples):
    trace_segment_length = record.shape[1]
    count_of_shots = shot_fire_samples.shape[0]
    dft_rows = dft_table(WIN)
    sample_offsets = shot_fire_samples - lax.axis_index("shot") * trace_segment_length
    head_rows = record[:, :WIN]
    rim_rows = shifted(head_rows, "shot", -1)
    extended = jnp.concatenate([record, rim_rows], axis=1)
    trace_spectra = local_spectra(extended, sample_offsets, dft_rows)
    trace_spectra = trace_spectra.astype(jnp.bfloat16)
    all_receivers = lax.all_gather(trace_spectra, "rcv", axis=2, tiled=True)
    total_shots = count_of_shots * lax.axis_size("shot")
    row_side = lax.all_gather(trace_spectra, "shot", axis=0, tiled=True)
    column_side = lax.all_to_all(all_receivers, "shot", split_axis=2, concat_axis=0, tiled=True)
    result = gram_terms(row_side, column_side)
    return result / total_shots


LANES = 128
HALF = 16
GROUP = 8
PIECES = 4
MESH = pl.DeviceIdType.MESH


def lane_fields(shape):
    lane = lax.broadcasted_iota(jnp.int32, shape, len(shape) - 1)
    return lane // 16 % 4, lane // 8 % 2, lane // 64 * 8 + lane % 8


def rotated(lag, quarter):
    freq, part, _ = lane_fields((1, LANES))
    bins = jnp.full((1, LANES), freq_bins[0], jnp.int32)
    for f in range(1, len(freq_bins)):
        bins = jnp.where(freq == f, freq_bins[f], bins)
    turn = (lag & (SPACING - 1)) * bins + (part * quarter[0] + quarter[1]) * (WIN // 4)
    turn = ((turn + WIN // 2) & (WIN - 1)) - WIN // 2
    x = (math.pi / WIN) * turn.astype(jnp.float32)
    y = x * x
    series = 1.0 / math.factorial(13)
    for k in (11, 9, 7, 5, 3, 1):
        series = series * y + (-1.0) ** (k // 2) / math.factorial(k)
    half_sine = x * series
    return 1.0 - 2.0 * half_sine * half_sine


def kernel(
    n, ncol, fire_hbm, rec_ref, out_ref,
    fire_ref, fire_sem, rec, joff, poff, wave, mask, tm0, tmc, tm1, tmf, rim_out, rim_in, gat, col, rmat,
    rec_sem, jit_sem, rim_sem, ring_send, share_send, ring_recv, share_recv, col_send, col_recv,
):
    me = lax.axis_index("shot")
    mj = lax.axis_index("rcv")
    rows = rec.shape[0]
    fold = rows // 2
    span = GROUP * SPACING
    chips = n // 2
    nz = chips // 2
    half = chips // 2
    reach = WIN // SPACING
    core = me % 2
    chip = me // 2
    z, y = chip // 2, chip % 2
    pos = jnp.where(y == 0, z, chips - 1 - z)

    def chip_at(position):
        q = (position + 2 * chips) % chips
        second = q >= nz
        zz = jnp.where(second, chips - 1 - q, q)
        return zz * 2 + jnp.where(second, 1, 0)

    ahead = (chip_at(pos + 1), chip_at(pos - 1))
    pair = chip * 2 + (1 - core)
    has_prev, has_next = me > 0, me < n - 1
    prev, nxt = jnp.maximum(me - 1, 0), jnp.minimum(me + 1, n - 1)

    def load(g):
        part = pl.ds(g * span, span)
        return pltpu.make_async_copy(rec_ref.at[:, part], rec.at[:, part], rec_sem.at[g])

    fires = pltpu.make_async_copy(fire_hbm, fire_ref, fire_sem)
    fires.start()
    for g in range(4):
        load(g).start()

    barrier = pltpu.get_barrier_semaphore()

    def greet(other, column):
        pl.semaphore_signal(barrier, inc=1, device_id=(other, column), device_id_type=MESH)

    pl.when(has_prev)(lambda: greet(prev, mj))
    pl.when(has_next)(lambda: greet(nxt, mj))
    greet(pair, mj)
    for other in ahead:
        greet(other * 2 + core, mj)
    for other in (chip, *ahead):
        for which in range(2):
            greet(other * 2 + which, 1 - mj)
    greeted = 9 + has_prev.astype(jnp.int32) + has_next.astype(jnp.int32)

    freq, part_of, shot_lane = lane_fields((1, LANES))
    lower_lanes = lax.broadcasted_iota(jnp.int32, (1, LANES), 1) < LANES // 2
    row_index = lax.broadcasted_iota(jnp.int32, (SPACING, LANES), 0)
    wave[0] = rotated(row_index, (1, 0)) * (1.0 / math.sqrt(WIN))
    wave[1] = rotated(row_index, (1, -1)) * (1.0 / math.sqrt(WIN))
    for rel in range(3 * GROUP):
        order = rel - lane_fields((16, LANES))[2]
        early = (order >= 0) & (order < reach)
        late = (order >= 1) & (order <= reach)
        mask[0, rel] = early.astype(jnp.float32).astype(jnp.bfloat16)
        mask[1, rel] = late.astype(jnp.float32).astype(jnp.bfloat16)
    out_ref[...] = jnp.zeros_like(out_ref)
    fires.wait()
    jitters = []
    for h in range(2):
        row = jnp.zeros((1, LANES), jnp.int32)
        for s in range(HALF):
            row = jnp.where(shot_lane == s, fire_ref[h * HALF + s], row)
        jitters.append(row & (SPACING - 1))
    joff[...] = jnp.broadcast_to(jitters[1], joff.shape)

    @pl.when(me == 0)
    def _():
        poff[...] = jnp.zeros_like(poff)

    jitter = pltpu.make_async_remote_copy(
        joff, poff, jit_sem.at[0], jit_sem.at[1], device_id=(nxt, mj), device_id_type=MESH
    )
    rim = pltpu.make_async_remote_copy(
        rim_out, rim_in, rim_sem.at[0], rim_sem.at[1], device_id=(prev, mj), device_id_type=MESH
    )

    def fill(start, places):
        turned = rotated(start, (0, 0)), rotated(start, (0, -1))
        for c in range(SPACING // 16):
            part = slice(c * 16, (c + 1) * 16)
            value = wave[0, part] * turned[0] + wave[1, part] * turned[1]
            inside = lax.broadcasted_iota(jnp.int32, (16, LANES), 0) + c * 16 >= start
            early = jnp.where(inside, value, 0.0).astype(jnp.bfloat16)
            late = jnp.where(inside, 0.0, value).astype(jnp.bfloat16)
            for rel, (ref, block, lanes) in places.items():
                at = slice(block * SPACING + c * 16, block * SPACING + (c + 1) * 16)
                ref[at, lanes] = early * mask[0, rel] + late * mask[1, rel]

    low, high = slice(0, LANES), slice(LANES, 2 * LANES)

    def two_dots(block, count, ref, first):
        parts = []
        for k in range(2):
            b, f = block + k * count, first + k * count
            parts.append(
                jnp.dot(
                    rec[:, b * SPACING : (b + count) * SPACING],
                    ref[f * SPACING : (f + count) * SPACING, :],
                    preferred_element_type=jnp.float32,
                )
            )
        return parts[0] + parts[1]

    def folded(value, second):
        top, bottom = value[:fold], value[fold:]
        if second:
            return jnp.where(lower_lanes, pltpu.roll(top, LANES // 2, 1), bottom)
        return jnp.where(lower_lanes, top, pltpu.roll(bottom, LANES // 2, 1))

    def ring(src, p, d):
        return pltpu.make_async_remote_copy(
            gat.at[src, p], gat.at[src, p], ring_send.at[d], ring_recv.at[src // 2, p],
            device_id=(ahead[d] * 2 + core, mj), device_id_type=MESH,
        )

    def share(src, p):
        return pltpu.make_async_remote_copy(
            gat.at[src, p], gat.at[src, p], share_send, share_recv.at[src // 2],
            device_id=(pair, mj), device_id_type=MESH,
        )

    def column_rows(target):
        home = target * 2 * ncol // rows
        first = target * 2 * ncol - home * rows
        top = first // fold
        return home == mj, top, pl.multiple_of(first - top * fold, 16)

    def send_col(src, p, target, sem):
        mine, top, first = column_rows(target)
        wanted = mine & (top == p) if p < 2 else mine

        @pl.when(wanted)
        def _():
            for which in range(2):
                pltpu.make_async_remote_copy(
                    gat.at[src, p, pl.ds(first + which * ncol, ncol), :], col.at[src, max(p - 1, 0)],
                    col_send.at[sem], col_recv.at[src],
                    device_id=(target * 2 + which, 1 - mj), device_id_type=MESH,
                ).start()

    def hops(p, d):
        return half if p % 2 == d else half - 1

    def source(t, d, which):
        return chip_at(pos - t if d == 0 else pos + t) * 2 + which

    def send_own(p):
        for d in (p % 2, 1 - p % 2):
            ring(me, p, d).start()

    def spread(src, p):
        share(src, p).start()
        send_col(src, p, chip, 0)

    def arrive(t, p):
        for d in (p % 2, 1 - p % 2):
            if t > hops(p, d):
                continue
            src = source(t, d, core)
            ring(src, p, d).wait_recv()
            if t < hops(p, d):
                ring(src, p, d).start()
            if t == half - 1 and hops(p, d) == half:
                send_col(src, p, ahead[d], 1 + p)
            if t < half:
                spread(src, p)
            else:
                share(src, p).start()

    provider, col_top, col_first = column_rows(chip)
    own_first = pl.multiple_of(col_first + core * ncol, 16)

    def take(buffer, sem):
        pltpu.make_async_copy(buffer, buffer, sem).wait()

    def gram(src, shared):
        if shared:
            take(gat.at[src], share_recv.at[src // 2])

        @pl.when(provider)
        def _():
            for k, p in enumerate((col_top, 2, 3)):
                col[src, k] = gat[src, p, pl.ds(own_first, ncol), :]

        pl.when(jnp.logical_not(provider))(lambda: take(col.at[src], col_recv.at[src]))
        xa, xb, xc = (col[src, k].astype(jnp.float32) for k in range(3))
        top = col_top == 0
        xb = jnp.where(top, xb, pltpu.roll(xb, LANES // 2, 1))
        xc = jnp.where(top, pltpu.roll(xc, LANES // 2, 1), xc)
        for h, x in enumerate((xa, jnp.where(lower_lanes, xb, xc))):
            swapped = jnp.where(part_of == 0, pltpu.roll(x, LANES - 8, 1), -pltpu.roll(x, 8, 1))
            for ri, value in enumerate((x, swapped)):
                for f in range(4):
                    rmat[pl.ds((ri * 4 + f) * ncol, ncol), h * LANES : (h + 1) * LANES] = jnp.where(
                        freq == f, value, 0.0
                    ).astype(jnp.bfloat16)
        b, c = gat[src, 2], gat[src, 3]
        k = LANES // 2
        left = jnp.concatenate(
            [
                jnp.concatenate([gat[src, 0], b[:, :k], c[:, :k]], axis=1),
                jnp.concatenate([gat[src, 1], b[:, k:], c[:, k:]], axis=1),
            ],
            axis=0,
        )
        out_ref[...] += lax.dot_general(
            rmat[...], left, (((1,), (1,)), ((), ())), preferred_element_type=jnp.float32
        )

    def gram_step(t):
        for which in range(2):
            for d in range(2):
                if d == 1 and t in (0, half):
                    continue
                src = source(t, d, core if which == 0 else 1 - core)
                gram(src, which == 1)

    fill(jitters[0], {r: (tm0, r, low) for r in range(16)})
    fill(jitters[0], {16 + r: (tmc, r, low) for r in range(8)})
    fill(jitters[1], {r: (tmc, r, high) for r in range(8)} | {8 + r: (tm1, r, low) for r in range(8)})
    pl.semaphore_wait(barrier, greeted)
    pl.when(has_next)(jitter.start)
    for g in range(3):
        load(g).wait()
    first_half = two_dots(0, 4, tm0, 0) + two_dots(8, 4, tm0, 8)
    middle = two_dots(16, 4, tmc, 0)
    first_half = (first_half + middle[:, :LANES]).astype(jnp.bfloat16)
    for p in range(2):
        gat[me, p] = first_half[p * fold : (p + 1) * fold]
    for p in range(2):
        send_own(p)
    load(3).wait()
    second_half = middle[:, LANES:] + two_dots(24, 4, tm1, 0)
    gat[me, 2] = folded(second_half, False).astype(jnp.bfloat16)
    pl.when(has_prev)(jitter.wait_recv)
    fill(poff[0:1, :], {16 + r: (tmf, r, low) for r in range(8)})
    rim_out[...] = folded(two_dots(0, 4, tmf, 0), True).astype(jnp.bfloat16)
    pl.when(has_prev)(rim.start)
    send_own(2)
    for p in range(3):
        spread(me, p)
    edge = folded(second_half, True)

    def finish():
        pl.when(has_next)(rim.wait_recv)
        outer = jnp.where(has_next, rim_in[...].astype(jnp.float32), 0.0)
        gat[me, 3] = (edge + outer).astype(jnp.bfloat16)
        send_own(3)
        spread(me, 3)

    pl.when(core == 0)(finish)
    for p in range(2):
        arrive(1, p)
    pl.when(core == 1)(finish)
    arrive(1, 2)
    gram_step(0)
    arrive(1, 3)
    for t in range(2, half + 1):
        for p in range(3):
            arrive(t, p)
        gram_step(t - 1)
        arrive(t, 3)
    gram_step(half)

    out_ref[...] *= 1.0 / (n * 2 * HALF)
    pl.when(has_next)(jitter.wait_send)
    pl.when(has_prev)(rim.wait_send)
    for d in range(2):
        whole, rest = divmod(sum(hops(p, d) for p in range(PIECES)), PIECES)
        take(gat.at[pl.ds(0, whole)], ring_send.at[d])
        if rest:
            take(gat.at[0, pl.ds(0, rest)], ring_send.at[d])
    take(gat.at[pl.ds(0, chips)], share_send)
    pl.when(provider)(lambda: take(col.at[pl.ds(0, 2 * (chips - 1))], col_send.at[0]))
    for p in range(PIECES):
        mine, top, _ = column_rows(ahead[p % 2])
        wanted = mine & (top == p) if p < 2 else mine
        pl.when(wanted)(lambda p=p: take(col.at[0, pl.ds(0, 2)], col_send.at[1 + p]))


def fused_device(n, ncol, record, shot_fire_samples):
    rows, length = record.shape
    chips = n // 2
    shot_fire_samples = pltpu.with_memory_space_constraint(shot_fire_samples, pltpu.HBM)
    gram = pl.pallas_call(
        functools.partial(kernel, n, ncol),
        out_shape=jax.ShapeDtypeStruct((8 * ncol, rows), jnp.float32),
        in_specs=[
            pl.BlockSpec(memory_space=pltpu.HBM),
            pl.BlockSpec(memory_space=pltpu.HBM),
        ],
        out_specs=pl.BlockSpec(memory_space=pltpu.VMEM),
        scratch_shapes=[
            pltpu.SMEM(shot_fire_samples.shape, jnp.int32),
            pltpu.SemaphoreType.DMA,
            pltpu.VMEM((rows, length), jnp.bfloat16),
            pltpu.VMEM((8, LANES), jnp.int32),
            pltpu.VMEM((8, LANES), jnp.int32),
            pltpu.VMEM((2, SPACING, LANES), jnp.float32),
            pltpu.VMEM((2, 3 * GROUP, 16, LANES), jnp.bfloat16),
            pltpu.VMEM((2 * GROUP * SPACING, LANES), jnp.bfloat16),
            pltpu.VMEM((GROUP * SPACING, 2 * LANES), jnp.bfloat16),
            pltpu.VMEM((GROUP * SPACING, LANES), jnp.bfloat16),
            pltpu.VMEM((GROUP * SPACING, LANES), jnp.bfloat16),
            pltpu.VMEM((rows // 2, LANES), jnp.bfloat16),
            pltpu.VMEM((rows // 2, LANES), jnp.bfloat16),
            pltpu.VMEM((n, PIECES, rows // 2, LANES), jnp.bfloat16),
            pltpu.VMEM((n, 3, ncol, LANES), jnp.bfloat16),
            pltpu.VMEM((8 * ncol, 2 * LANES), jnp.bfloat16),
            pltpu.SemaphoreType.DMA((length // (GROUP * SPACING),)),
            pltpu.SemaphoreType.DMA((2,)),
            pltpu.SemaphoreType.DMA((2,)),
            pltpu.SemaphoreType.DMA((2,)),
            pltpu.SemaphoreType.DMA,
            pltpu.SemaphoreType.DMA((chips, PIECES)),
            pltpu.SemaphoreType.DMA((chips,)),
            pltpu.SemaphoreType.DMA((1 + PIECES,)),
            pltpu.SemaphoreType.DMA((n,)),
        ],
        compiler_params=pltpu.CompilerParams(
            collective_id=0, has_side_effects=True, vmem_limit_bytes=50 * 1024 * 1024
        ),
    )(shot_fire_samples, record)
    return gram.reshape(2, 4, ncol, rows).transpose(0, 1, 3, 2)


def whole_step(n, receivers, record, shot_fire_samples):
    rows, length = record.shape
    shots = shot_fire_samples.shape[0]
    ncol = receivers // n
    fits = (
        receivers == 2 * rows and ncol % 16 == 0 and rows % (4 * ncol) == 0
        and shots == 2 * HALF and length == shots * SPACING and n % 8 == 0
    )
    if fits:
        return fused_device(n, ncol, record, shot_fire_samples)
    return per_device(record, shot_fire_samples)


def solution(mesh):
    def step(record, shot_fire_samples):
        body = functools.partial(whole_step, mesh.shape["shot"], record.shape[0])
        return jax.shard_map(
            body,
            mesh=mesh,
            in_specs=(P("rcv", "shot"), P("shot")),
            out_specs=P(None, None, "rcv", "shot"),
            check_vma=False,
        )(record, shot_fire_samples)

    return step
```

time: 33.4 us -> 30.4 us (0.910); the launches traced: 33.3 us -> 29.9 us
  Pallas kernels: 32.4 us -> 29.1 us
    pallas_call x1, Pallas kernels: 32.4 us -> 29.1 us  [fused_device(): pl.pallas_call(functools.partial(kernel, n, ncol), out_shape=jax.ShapeDty...]
where the time goes in v2:
time: 30.4 us; the launch traced here: 29.9 us
  Pallas kernels  29.1 us (96%)
  local copies, waits for them, and re-layouts  0.82 us (3%)
    pallas_call x1, Pallas kernels, fused_device(): pl.pallas_call(functools.partial(kernel, n, ncol), out_shape=jax.ShapeDty...  29.1 us
    unnamed x1, local copies, waits for them, and re-layouts  0.82 us

profile of v2, /device:TPU:0, one launch (start us, length us, event | category | flops | bytes accessed | tf_op | source)
XLA Modules:
  0.0 29.9 jit_solution(9743667085134801005)
XLA Ops:
  0.0 29.1 %shard_map.28 = f32[384,384]{1,0:T(8,128)S(1)} custom-call(s32[32]{0:T(128)} %fire_hbm.1, bf16[384,8192]{1,0:T(8,128)(2,1)} %rec_ref.1), custom_call_target="tpu_custom_call" | custom-call | tf_op jit(solution)/shard_map/pallas_call | solution.py:420
  29.1 0.8 %copy.4 = f32[2,4,384,48]{2,3,1,0:T(8,128)} copy(f32[2,4,384,48]{2,3,1,0:T(8,128)S(1)} %bitcast.3) | data formatting | bytes 1179648

commit v3 on v2

--- a/solution.py
+++ b/solution.py
@@ -172,16 +172,19 @@
     greet(pair, mj)
     for other in ahead:
         greet(other * 2 + core, mj)
-    for other in (chip, *ahead):
-        for which in range(2):
-            greet(other * 2 + which, 1 - mj)
-    greeted = 9 + has_prev.astype(jnp.int32) + has_next.astype(jnp.int32)
+    for which in range(2):
+        greet(chip * 2 + which, 1 - mj)
+    greeted = 5 + has_prev.astype(jnp.int32) + has_next.astype(jnp.int32)
 
     freq, part_of, shot_lane = lane_fields((1, LANES))
     lower_lanes = lax.broadcasted_iota(jnp.int32, (1, LANES), 1) < LANES // 2
-    row_index = lax.broadcasted_iota(jnp.int32, (SPACING, LANES), 0)
-    wave[0] = rotated(row_index, (1, 0)) * (1.0 / math.sqrt(WIN))
-    wave[1] = rotated(row_index, (1, -1)) * (1.0 / math.sqrt(WIN))
+    row_index = lax.broadcasted_iota(jnp.int32, (16, LANES), 0)
+    fine = [rotated(row_index, (1, quarter)) * (1.0 / math.sqrt(WIN)) for quarter in (0, -1)]
+    coarse = [rotated(row_index * 16, (0, quarter)) for quarter in (0, -1)]
+    for c in range(SPACING // 16):
+        at, (cosine, sine) = slice(c * 16, (c + 1) * 16), (turn[c : c + 1] for turn in coarse)
+        wave[0, at] = fine[0] * cosine - fine[1] * sine
+        wave[1, at] = fine[1] * cosine + fine[0] * sine
     for rel in range(3 * GROUP):
         order = rel - lane_fields((16, LANES))[2]
         early = (order >= 0) & (order < reach)
@@ -287,20 +290,17 @@
         share(src, p).start()
         send_col(src, p, chip, 0)
 
-    def arrive(t, p):
-        for d in (p % 2, 1 - p % 2):
-            if t > hops(p, d):
-                continue
-            src = source(t, d, core)
-            ring(src, p, d).wait_recv()
-            if t < hops(p, d):
-                ring(src, p, d).start()
-            if t == half - 1 and hops(p, d) == half:
-                send_col(src, p, ahead[d], 1 + p)
-            if t < half:
-                spread(src, p)
-            else:
-                share(src, p).start()
+    def arrive(t, p, d):
+        src = source(t, d, core)
+        ring(src, p, d).wait_recv()
+        if t < hops(p, d):
+            ring(src, p, d).start()
+        if t == half - 1 and hops(p, d) == half:
+            send_col(src, p, ahead[d], 1 + p)
+        if t < half:
+            spread(src, p)
+        else:
+            share(src, p).start()
 
     provider, col_top, col_first = column_rows(chip)
     own_first = pl.multiple_of(col_first + core * ncol, 16)
@@ -308,47 +308,61 @@
     def take(buffer, sem):
         pltpu.make_async_copy(buffer, buffer, sem).wait()
 
-    def gram(src, shared):
-        if shared:
-            take(gat.at[src], share_recv.at[src // 2])
+    def gram(sources, last=False):
+        for src, shared in sources:
+            if shared:
+                take(gat.at[src], share_recv.at[src // 2])
 
         @pl.when(provider)
         def _():
-            for k, p in enumerate((col_top, 2, 3)):
-                col[src, k] = gat[src, p, pl.ds(own_first, ncol), :]
-
-        pl.when(jnp.logical_not(provider))(lambda: take(col.at[src], col_recv.at[src]))
-        xa, xb, xc = (col[src, k].astype(jnp.float32) for k in range(3))
-        top = col_top == 0
-        xb = jnp.where(top, xb, pltpu.roll(xb, LANES // 2, 1))
-        xc = jnp.where(top, pltpu.roll(xc, LANES // 2, 1), xc)
-        for h, x in enumerate((xa, jnp.where(lower_lanes, xb, xc))):
-            swapped = jnp.where(part_of == 0, pltpu.roll(x, LANES - 8, 1), -pltpu.roll(x, 8, 1))
-            for ri, value in enumerate((x, swapped)):
-                for f in range(4):
-                    rmat[pl.ds((ri * 4 + f) * ncol, ncol), h * LANES : (h + 1) * LANES] = jnp.where(
-                        freq == f, value, 0.0
-                    ).astype(jnp.bfloat16)
-        b, c = gat[src, 2], gat[src, 3]
-        k = LANES // 2
-        left = jnp.concatenate(
-            [
-                jnp.concatenate([gat[src, 0], b[:, :k], c[:, :k]], axis=1),
-                jnp.concatenate([gat[src, 1], b[:, k:], c[:, k:]], axis=1),
-            ],
-            axis=0,
+            for src, _ in sources:
+                for k, p in enumerate((col_top, 2, 3)):
+                    col[src, k] = gat[src, p, pl.ds(own_first, ncol), :]
+
+        @pl.when(jnp.logical_not(provider))
+        def _():
+            for src, _ in sources:
+                take(col.at[src], col_recv.at[src])
+
+        lefts = []
+        for slot, (src, _) in enumerate(sources):
+            xa, xb, xc = (col[src, k].astype(jnp.float32) for k in range(3))
+            top = col_top == 0
+            xb = jnp.where(top, xb, pltpu.roll(xb, LANES // 2, 1))
+            xc = jnp.where(top, pltpu.roll(xc, LANES // 2, 1), xc)
+            for h, x in enumerate((xa, jnp.where(lower_lanes, xb, xc))):
+                at = slice((2 * slot + h) * LANES, (2 * slot + h + 1) * LANES)
+                swapped = jnp.where(part_of == 0, pltpu.roll(x, LANES - 8, 1), -pltpu.roll(x, 8, 1))
+                for ri, value in enumerate((x, swapped)):
+                    for f in range(4):
+                        rmat[pl.ds((ri * 4 + f) * ncol, ncol), at] = jnp.where(
+                            freq == f, value, 0.0
+                        ).astype(jnp.bfloat16)
+            b, c = gat[src, 2], gat[src, 3]
+            k = LANES // 2
+            lefts.append(
+                jnp.concatenate(
+                    [
+                        jnp.concatenate([gat[src, 0], b[:, :k], c[:, :k]], axis=1),
+                        jnp.concatenate([gat[src, 1], b[:, k:], c[:, k:]], axis=1),
+                    ],
+                    axis=0,
+                )
+            )
+        total = out_ref[...] + lax.dot_general(
+            rmat[:, : 2 * LANES * len(sources)], jnp.concatenate(lefts, axis=1),
+            (((1,), (1,)), ((), ())), preferred_element_type=jnp.float32,
         )
-        out_ref[...] += lax.dot_general(
-            rmat[...], left, (((1,), (1,)), ((), ())), preferred_element_type=jnp.float32
-        )
-
-    def gram_step(t):
-        for which in range(2):
+        out_ref[...] = total * (1.0 / (n * 2 * HALF)) if last else total
+
+    def grams(t):
+        found = []
+        for other in range(2):
             for d in range(2):
                 if d == 1 and t in (0, half):
                     continue
-                src = source(t, d, core if which == 0 else 1 - core)
-                gram(src, which == 1)
+                found.append((source(t, d, 1 - core if other else core), other == 1))
+        return found
 
     fill(jitters[0], {r: (tm0, r, low) for r in range(16)})
     fill(jitters[0], {16 + r: (tmc, r, low) for r in range(8)})
@@ -369,7 +383,7 @@
     gat[me, 2] = folded(second_half, False).astype(jnp.bfloat16)
     pl.when(has_prev)(jitter.wait_recv)
     fill(poff[0:1, :], {16 + r: (tmf, r, low) for r in range(8)})
-    rim_out[...] = folded(two_dots(0, 4, tmf, 0), True).astype(jnp.bfloat16)
+    rim_out[...] = folded(out_ref[:, :LANES] + two_dots(0, 4, tmf, 0), True).astype(jnp.bfloat16)
     pl.when(has_prev)(rim.start)
     send_own(2)
     for p in range(3):
@@ -383,21 +397,27 @@
         send_own(3)
         spread(me, 3)
 
+    def arrivals(t, p):
+        for d in (p % 2, 1 - p % 2):
+            if t <= hops(p, d):
+                arrive(t, p, d)
+
     pl.when(core == 0)(finish)
     for p in range(2):
-        arrive(1, p)
+        arrivals(1, p)
     pl.when(core == 1)(finish)
-    arrive(1, 2)
-    gram_step(0)
-    arrive(1, 3)
+    arrivals(1, 2)
+    gram(grams(0))
+    arrivals(1, 3)
     for t in range(2, half + 1):
         for p in range(3):
-            arrive(t, p)
-        gram_step(t - 1)
-        arrive(t, 3)
-    gram_step(half)
-
-    out_ref[...] *= 1.0 / (n * 2 * HALF)
+            arrivals(t, p)
+        gram(grams(t - 1))
+        arrivals(t, 3)
+    own, other = grams(half)
+    gram([own])
+    gram([other], last=True)
+
     pl.when(has_next)(jitter.wait_send)
     pl.when(has_prev)(rim.wait_send)
     for d in range(2):
@@ -441,7 +461,7 @@
             pltpu.VMEM((rows // 2, LANES), jnp.bfloat16),
             pltpu.VMEM((n, PIECES, rows // 2, LANES), jnp.bfloat16),
             pltpu.VMEM((n, 3, ncol, LANES), jnp.bfloat16),
-            pltpu.VMEM((8 * ncol, 2 * LANES), jnp.bfloat16),
+            pltpu.VMEM((8 * ncol, 8 * LANES), jnp.bfloat16),
             pltpu.SemaphoreType.DMA((length // (GROUP * SPACING),)),
             pltpu.SemaphoreType.DMA((2,)),
             pltpu.SemaphoreType.DMA((2,)),

time: 30.4 us -> 28.8 us (0.947)
  Pallas kernels: 29.1 us -> 27.5 us
    pallas_call x1, Pallas kernels: 29.1 us -> 27.5 us  [fused_device(): pl.pallas_call(functools.partial(kernel, n, ncol), out_shape=jax.ShapeDty...]
where the time goes in v3:
time: 28.8 us; the launch traced here: 28.4 us
  Pallas kernels  27.5 us (95%)
  local copies, waits for them, and re-layouts  0.82 us (3%)
    pallas_call x1, Pallas kernels, fused_device(): pl.pallas_call(functools.partial(kernel, n, ncol), out_shape=jax.ShapeDty...  27.5 us
    unnamed x1, local copies, waits for them, and re-layouts  0.82 us

profile of v3, /device:TPU:0, one launch (start us, length us, event | category | flops | bytes accessed | tf_op | source)
XLA Modules:
  0.0 28.4 jit_solution(16139836064064984648)
XLA Ops:
  0.0 27.5 %shard_map.28 = f32[384,384]{1,0:T(8,128)S(1)} custom-call(s32[32]{0:T(128)} %fire_hbm.1, bf16[384,8192]{1,0:T(8,128)(2,1)} %rec_ref.1), custom_call_target="tpu_custom_call" | custom-call | tf_op jit(solution)/shard_map/pallas_call | solution.py:440
  27.6 0.8 %copy.4 = f32[2,4,384,48]{2,3,1,0:T(8,128)} copy(f32[2,4,384,48]{2,3,1,0:T(8,128)S(1)} %bitcast.3) | data formatting | bytes 1179648

commit v4 on v3

--- a/solution.py
+++ b/solution.py
@@ -121,6 +121,62 @@
         series = series * y + (-1.0) ** (k // 2) / math.factorial(k)
     half_sine = x * series
     return 1.0 - 2.0 * half_sine * half_sine
+
+
+EVENTS = (
+    ('own', 0),
+    ('arr', 1, 0, 1),
+    ('arr', 1, 0, 0),
+    ('own', 1),
+    ('arr', 1, 2, 0),
+    ('arr', 1, 1, 1),
+    ('arr', 1, 1, 0),
+    ('arr', 1, 3, 1),
+    ('arr', 2, 0, 0),
+    ('arr', 1, 2, 1),
+    ('arr', 1, 3, 0),
+    ('arr', 2, 0, 1),
+    ('arr', 2, 1, 1),
+    ('gram', ((0, 0, 1),)),
+    ('arr', 2, 2, 0),
+    ('arr', 2, 1, 0),
+    ('gram', ((0, 0, 0),)),
+    ('arr', 2, 3, 1),
+    ('arr', 2, 3, 0),
+    ('arr', 2, 2, 1),
+    ('arr', 3, 0, 1),
+    ('arr', 3, 0, 0),
+    ('arr', 3, 1, 1),
+    ('arr', 3, 2, 0),
+    ('gram', ((2, 0, 0),)),
+    ('arr', 3, 3, 1),
+    ('gram', ((1, 0, 1), (1, 1, 0), (2, 0, 1), (2, 1, 0))),
+    ('arr', 3, 2, 1),
+    ('arr', 3, 1, 0),
+    ('arr', 3, 3, 0),
+    ('gram', ((1, 1, 1), (2, 1, 1), (1, 0, 0))),
+    ('arr', 4, 0, 0),
+    ('gram', ((3, 1, 0), (3, 1, 1))),
+    ('arr', 4, 1, 1),
+    ('arr', 4, 2, 0),
+    ('arr', 4, 3, 1),
+    ('gram', ((4, 0, 0), (3, 0, 0), (3, 0, 1))),
+    ('gram', ((4, 0, 1),)),
+)
+
+
+def plain_events(half):
+    def legs(t, p):
+        return [("arr", t, p, d) for d in (p % 2, 1 - p % 2) if t <= (half if p % 2 == d else half - 1)]
+
+    def sums(t):
+        sides = (0,) if t in (0, half) else (0, 1)
+        return tuple((t, d, other) for other in range(2) for d in sides)
+
+    events = [("own", 0), *legs(1, 0), *legs(1, 1), ("own", 1), *legs(1, 2), ("gram", sums(0)), *legs(1, 3)]
+    for t in range(2, half + 1):
+        events += [*legs(t, 0), *legs(t, 1), *legs(t, 2), ("gram", sums(t - 1)), *legs(t, 3)]
+    return [*events, *(("gram", (one,)) for one in sums(half))]
 
 
 def kernel(
@@ -159,7 +215,7 @@
 
     fires = pltpu.make_async_copy(fire_hbm, fire_ref, fire_sem)
     fires.start()
-    for g in range(4):
+    for g in range(3):
         load(g).start()
 
     barrier = pltpu.get_barrier_semaphore()
@@ -367,11 +423,14 @@
     fill(jitters[0], {r: (tm0, r, low) for r in range(16)})
     fill(jitters[0], {16 + r: (tmc, r, low) for r in range(8)})
     fill(jitters[1], {r: (tmc, r, high) for r in range(8)} | {8 + r: (tm1, r, low) for r in range(8)})
+    load(3).start()
     pl.semaphore_wait(barrier, greeted)
     pl.when(has_next)(jitter.start)
-    for g in range(3):
+    load(0).wait()
+    first_half = two_dots(0, 4, tm0, 0)
+    for g in (1, 2):
         load(g).wait()
-    first_half = two_dots(0, 4, tm0, 0) + two_dots(8, 4, tm0, 8)
+    first_half = first_half + two_dots(8, 4, tm0, 8)
     middle = two_dots(16, 4, tmc, 0)
     first_half = (first_half + middle[:, :LANES]).astype(jnp.bfloat16)
     for p in range(2):
@@ -402,21 +461,15 @@
             if t <= hops(p, d):
                 arrive(t, p, d)
 
-    pl.when(core == 0)(finish)
-    for p in range(2):
-        arrivals(1, p)
-    pl.when(core == 1)(finish)
-    arrivals(1, 2)
-    gram(grams(0))
-    arrivals(1, 3)
-    for t in range(2, half + 1):
-        for p in range(3):
-            arrivals(t, p)
-        gram(grams(t - 1))
-        arrivals(t, 3)
-    own, other = grams(half)
-    gram([own])
-    gram([other], last=True)
+    events = EVENTS if half == 4 else plain_events(half)
+    for event in events:
+        if event[0] == "own":
+            pl.when(core == event[1])(finish)
+        elif event[0] == "arr":
+            arrive(*event[1:])
+        else:
+            group = [(source(t, d, 1 - core if other else core), other == 1) for t, d, other in event[1]]
+            gram(group, last=event is events[-1])
 
     pl.when(has_next)(jitter.wait_send)
     pl.when(has_prev)(rim.wait_send)

time: 28.8 us -> 27.6 us (0.958)
  Pallas kernels: 27.5 us -> 26.4 us
    pallas_call x1, Pallas kernels: 27.5 us -> 26.4 us  [fused_device(): pl.pallas_call(functools.partial(kernel, n, ncol), out_shape=jax.ShapeDty...]
where the time goes in v4:
time: 27.6 us; the launch traced here: 27.3 us
  Pallas kernels  26.4 us (96%)
  local copies, waits for them, and re-layouts  0.82 us (3%)
    pallas_call x1, Pallas kernels, fused_device(): pl.pallas_call(functools.partial(kernel, n, ncol), out_shape=jax.ShapeDty...  26.4 us
    unnamed x1, local copies, waits for them, and re-layouts  0.82 us

profile of v4, /device:TPU:0, one launch (start us, length us, event | category | flops | bytes accessed | tf_op | source)
XLA Modules:
  0.0 27.3 jit_solution(11699227257415022775)
XLA Ops:
  0.0 26.4 %shard_map.28 = f32[384,384]{1,0:T(8,128)S(1)} custom-call(s32[32]{0:T(128)} %fire_hbm.1, bf16[384,8192]{1,0:T(8,128)(2,1)} %rec_ref.1), custom_call_target="tpu_custom_call" | custom-call | tf_op jit(solution)/shard_map/pallas_call | solution.py:493
  26.4 0.8 %copy.4 = f32[2,4,384,48]{2,3,1,0:T(8,128)} copy(f32[2,4,384,48]{2,3,1,0:T(8,128)S(1)} %bitcast.3) | data formatting | bytes 1179648

commit v5 on v4

--- a/solution.py
+++ b/solution.py
@@ -422,7 +422,7 @@
 
     fill(jitters[0], {r: (tm0, r, low) for r in range(16)})
     fill(jitters[0], {16 + r: (tmc, r, low) for r in range(8)})
-    fill(jitters[1], {r: (tmc, r, high) for r in range(8)} | {8 + r: (tm1, r, low) for r in range(8)})
+    fill(jitters[1], {r: (tmc, r, high) for r in range(8)})
     load(3).start()
     pl.semaphore_wait(barrier, greeted)
     pl.when(has_next)(jitter.start)
@@ -438,6 +438,7 @@
     for p in range(2):
         send_own(p)
     load(3).wait()
+    fill(jitters[1], {8 + r: (tm1, r, low) for r in range(8)})
     second_half = middle[:, LANES:] + two_dots(24, 4, tm1, 0)
     gat[me, 2] = folded(second_half, False).astype(jnp.bfloat16)
     pl.when(has_prev)(jitter.wait_recv)

time: 27.6 us -> 27.6 us (level)
  no operation moved by 1% of the time
where the time goes in v5:
time: 27.6 us; the launch traced here: 27.2 us
  Pallas kernels  26.4 us (96%)
  local copies, waits for them, and re-layouts  0.82 us (3%)
    pallas_call x1, Pallas kernels, fused_device(): pl.pallas_call(functools.partial(kernel, n, ncol), out_shape=jax.ShapeDty...  26.4 us
    unnamed x1, local copies, waits for them, and re-layouts  0.82 us

profile of v5, /device:TPU:0, one launch (start us, length us, event | category | flops | bytes accessed | tf_op | source)
XLA Modules:
  0.0 27.2 jit_solution(12532821146959015479)
XLA Ops:
  0.0 26.4 %shard_map.28 = f32[384,384]{1,0:T(8,128)S(1)} custom-call(s32[32]{0:T(128)} %fire_hbm.1, bf16[384,8192]{1,0:T(8,128)(2,1)} %rec_ref.1), custom_call_target="tpu_custom_call" | custom-call | tf_op jit(solution)/shard_map/pallas_call | solution.py:494
  26.4 0.8 %copy.4 = f32[2,4,384,48]{2,3,1,0:T(8,128)} copy(f32[2,4,384,48]{2,3,1,0:T(8,128)S(1)} %bitcast.3) | data formatting | bytes 1179648
